TPU v7x, 512 devices: a whole 4x8x8 slice. The times are simulated.
512 devices in a mesh: panel: 2 (over x_hi), rad: 8 (over z), ang: 32 (over y, x_lo, core).
Axes of the slice: x: 4 (x_hi: 2, x_lo: 2; x = x_hi * 2 + x_lo), y: 8, z: 8, core: 2. Of those that a mesh axis runs over, the one named last changes fastest.
Arguments:
- adj_final: float32 [2, 7, 8, 256, 1536], P('panel', None, 'rad', 'ang'), may hold values from -6 to 6
- cond: float32 [2, 8, 256, 1536], P('panel', 'rad', 'ang'), may hold values from 0.5 to 1.5
- diffus: float32 [7], replicated, may hold values from 0.02 to 0.1
- couple: float32 [7, 7], replicated, may hold values from -0.1 to 0.1
- ghost_row: int32 [2, 4, 256], replicated, may hold values from 0 to 255
- ghost_col: int32 [2, 4, 256], replicated, may hold values from 0 to 1535
- ghost_wt: float32 [2, 4, 256], replicated, may hold values from 0.5 to 1.5
- obs_dest: int32 [2, 8, 8192, 1], P('panel', 'rad', 'ang'), may hold values from 0 to 31; in each aligned block of 256 rows (0 to 255, 256 to 511, ..., all dimensions but the last counted through in order) at most 16 rows name the same one
- obs_cell: int32 [2, 8, 4, 8192], P('panel', 'rad', None, 'ang'), may hold values from 0 to 12287
- obs_wt: float32 [2, 8, 4, 8192], P('panel', 'rad', None, 'ang'), may hold values from 0.2 to 1
- misfit: float32 [2, 8, 2, 8192], P('panel', 'rad', None, 'ang'), may hold values from -6 to 6
Outputs:
- adj_start: float32 [2, 7, 8, 256, 1536], P('panel', None, 'rad', 'ang')
Inputs may be any that keep to these rules, and one draw needn't show every extreme that they name: `obs_dest`: owner tile, within the observation's own panel, whose outermost layer holds it; among the 256 observations of one device at most 16 name one owner. `obs_cell`: row within the owner's tile times 1536 plus column.
All inputs are finite; a program needn't handle non-finite values.
Results may differ from a plain program's by a relative error of at most 0.000088.
Values sent between devices are 32-bit elements; how exact they have to be, the bound alone decides.
A program may use at most 64 MiB of HBM per device.

v0:
```python
import jax
import jax.numpy as jnp
from jax import lax
from jax.sharding import PartitionSpec as P


def swapped(x, axis, apart):
    return lax.ppermute(x, axis, [(i, i ^ 1 << apart) for i in range(lax.axis_size(axis))])


def extended(block, sides, width):
    for axis, dim in sides:
        count = lax.axis_size(axis)
        forward = [(i, i + 1) for i in range(count - 1)]
        backward = [(target, source) for source, target in forward]
        low = lax.ppermute(
            lax.slice_in_dim(block, block.shape[dim] - width, None, axis=dim), axis, forward
        )
        high = lax.ppermute(lax.slice_in_dim(block, 0, width, axis=dim), axis, backward)
        block = jnp.concatenate([low, block, high], axis=dim)
    return block


def deposit(inbox, cells_total):
    values = inbox[:8].reshape(2, -1)
    cells = inbox[8:].astype(jnp.int32).reshape(-1)
    dense = jnp.zeros((2, cells_total), jnp.float32)
    return dense.at[:, cells].add(values, mode="drop")


def route_obs(obs_dest, obs_cell, obs_wt, misfit, cells_total):
    target = obs_dest[0, 0, :, 0]
    count = target.shape[0]
    owners = lax.axis_size("ang")
    slots = 2 * count // owners
    onehot = (target[:, None] == jnp.arange(owners, dtype=jnp.int32)[None]).astype(jnp.int32)
    before = jnp.cumsum(onehot, axis=0) - onehot
    ranking = jnp.sum(before * onehot, axis=1)
    position = target * slots + ranking
    values = (misfit[0, 0][:, None, :] * obs_wt[0, 0][None]).reshape(8, count)
    payload = jnp.concatenate([values, obs_cell[0, 0].astype(jnp.float32)], axis=0)
    blank = jnp.concatenate(
        [
            jnp.zeros((8, owners * slots), jnp.float32),
            jnp.full((4, owners * slots), cells_total, jnp.float32),
        ],
        axis=0,
    )
    outbox = blank.at[:, position].set(payload)
    inbox = lax.all_to_all(outbox, "ang", split_axis=1, concat_axis=1, tiled=True)
    dense = deposit(inbox, cells_total)
    return lax.psum(dense, "rad")


def other_edges(edges):
    across = swapped(edges, "panel", 0)
    return lax.all_gather(across, "ang", axis=3, tiled=True)


def ghost_terms(scaled_own, row_start, central_rows, ghost_row, ghost_col, ghost_wt):
    fields, layers, tile_rows, columns = scaled_own.shape
    edges = jnp.stack([scaled_own[..., 0], scaled_own[..., -1]], axis=2)
    gathered = other_edges(edges)
    values = gathered[:, :, :, None, :] * ghost_wt[None, None]
    local_row = ghost_row - row_start
    inside = (local_row >= 0) & (local_row < central_rows)
    flat_index = jnp.where(inside, local_row * columns + ghost_col, central_rows * columns).reshape(
        -1
    )
    target = jnp.zeros((fields, layers, central_rows * columns), jnp.float32)
    target = target.at[:, :, flat_index].add(values.reshape(fields, layers, -1), mode="drop")
    return target.reshape(fields, layers, central_rows, columns)


def finish(padded, centre, ghost_add, source, couple, row_start, total_rows):
    middle = padded[:, 1:-1, 1:-1]
    lap = padded[:, 2:, 1:-1] + padded[:, :-2, 1:-1] + padded[:, 1:-1, 2:] + padded[:, 1:-1, :-2]
    west = jnp.pad(middle[..., :-1], ((0, 0), (0, 0), (0, 0), (1, 0)))
    east = jnp.pad(middle[..., 1:], ((0, 0), (0, 0), (0, 0), (0, 1)))
    lap = lap + west + east - 6.0 * middle
    coupled = jnp.einsum("ec,elrk->clrk", couple, centre, precision=lax.Precision.HIGHEST)
    updated = centre + lap + ghost_add + coupled
    updated = updated.at[3].add(source)
    global_rows = row_start + jnp.arange(centre.shape[2], dtype=jnp.int32)
    inside = ((global_rows >= 0) & (global_rows < total_rows)).astype(jnp.float32)
    return updated * inside[None, None, :, None]


def shallow_step(
    adjoint, coeff, source, couple, row_start, total_rows, ghost_row, ghost_col, ghost_wt
):
    scaled = coeff * adjoint
    padded = extended(scaled, (("rad", 1), ("ang", 2)), 1)
    ghost_add = ghost_terms(scaled, row_start, adjoint.shape[2], ghost_row, ghost_col, ghost_wt)
    return finish(padded, adjoint, ghost_add, source, couple, row_start, total_rows)


def body(
    adj_final,
    cond,
    diffus,
    couple,
    ghost_row,
    ghost_col,
    ghost_wt,
    obs_dest,
    obs_cell,
    obs_wt,
    misfit,
):
    adjoint = adj_final[0]
    conduct = cond[0]
    fields, layers, tile_rows, columns = adjoint.shape
    total_rows = tile_rows * lax.axis_size("ang")
    row_start = lax.axis_index("ang") * tile_rows
    outer = (lax.axis_index("rad") == lax.axis_size("rad") - 1).astype(jnp.float32)
    forcing = route_obs(obs_dest, obs_cell, obs_wt, misfit, tile_rows * columns)
    sources = []
    for moment in range(2):
        blank = jnp.zeros((layers, tile_rows, columns), jnp.float32)
        sources.append(
            blank.at[layers - 1].set(forcing[moment].reshape(tile_rows, columns) * outer)
        )
    coeff = diffus[:, None, None, None] * conduct[None]
    first = shallow_step(
        adjoint, coeff, sources[1], couple, row_start, total_rows, ghost_row, ghost_col, ghost_wt
    )
    final = shallow_step(
        first, coeff, sources[0], couple, row_start, total_rows, ghost_row, ghost_col, ghost_wt
    )
    return final[None]


def solution(mesh):
    placed = (
        P("panel", None, "rad", "ang", None),
        P("panel", "rad", "ang", None),
        P(),
        P(),
        P(),
        P(),
        P(),
        P("panel", "rad", "ang", None),
        P("panel", "rad", None, "ang"),
        P("panel", "rad", None, "ang"),
        P("panel", "rad", None, "ang"),
    )
    return jax.shard_map(
        body,
        mesh=mesh,
        in_specs=placed,
        out_specs=P("panel", None, "rad", "ang", None),
        check_vma=False,
    )
```

profile of v0, /device:TPU:1, one launch (start us, length us, event | category | flops | bytes accessed | tf_op | source)
XLA Modules:
  0.0 364.4 jit_solution(14950490070713340924)
XLA Ops:
  6.5 1.2 multiply_multiply_fusion.1
  7.8 1.3 collective-permute-start
  9.1 5.5 %collective-permute-start.1 = (f32[7,1,8,1536]{3,0,2,1:T(8,128)S(1)}, f32[7,1,8,1536]{3,0,2,1:T(8,128)S(1)}, u32[]{:S(2)}, u32[]{:S(2)}) collective-permute-start(f32[7,1,8,1536]{3,0,2,1:T(8,128)S(1)} %multiply_multiply_fusion.1), channel_id=1, source_target_pairs={{0,32},{32,64},{64,96},{96,128},{128,160},{160,192},{192,224},{1,3... | collective-permute-start | bytes 1032200 | tf_op jit(solution)/shard_map/ppermute | solution.py:16
  14.9 4.7 %collective-permute-start.4 = (f32[7,1,2,8]{3,2,0,1:T(2,128)S(1)}, f32[7,1,2,8]{3,2,0,1:T(2,128)S(1)}, u32[]{:S(2)}, u32[]{:S(2)}) collective-permute-start(f32[7,1,2,8]{3,2,0,1:T(2,128)S(1)} %pad_maximum_fusion.18), channel_id=1, source_target_pairs={{0,256},{256,0},{1,257},{257,1},{2,258},{258,2},{3,259},{259,3},{4... | collective-permute-start | bytes 1352 | tf_op jit(solution)/shard_map/ppermute | solution.py:8
  19.6 0.7 fusion.37
  20.3 0.6 reduce-window.6
  20.8 0.2 slice_reduce_fusion
  21.1 0.8 fusion.36
  21.8 0.7 compare_select_fusion.2
  22.5 0.9 copy.119
  23.5 0.7 broadcast_multiply_fusion
  24.2 0.7 convert_bitcast_fusion
  25.0 1.3 scatter_fusion
  26.3 0.3 copy.83
  26.5 0.8 reshape.458
  27.3 8.5 %all-to-all-start = ((f32[32,1,192]{2,1,0:T(1,128)}), f32[32,1,192]{2,1,0:T(1,128)S(1)}, u32[]{:S(2)}, u32[]{:S(2)}) async-start(f32[32,1,192]{2,1,0:T(1,128)} %reshape.458), calls=%async_computation | async-start | bytes 65536 | tf_op jit(solution)/shard_map/all_to_all | solution.py:50
  35.9 0.2 fusion.42
  36.1 0.7 add_select_fusion
  36.9 0.7 copy.108
  37.7 35.1 %all_gather.6 = f32[7,1,2,256]{0,2,1,3:T(2,128)S(1)} all-gather(f32[7,1,2,8]{0,2,1,3:T(2,128)S(1)} %copy.75), channel_id=1, replica_groups=mesh['panel'=2,'rad'=8,'ang'=32] {'ang'}, dimensions={3}, use_global_device_ids=true | all-gather | bytes 14784 | tf_op jit(solution)/shard_map/all_gather | solution.py:57
  72.8 15.5 %scatter_custom_fusion = f32[7,12288]{0,1:T(8,128)} fusion(s32[2048]{0:T(1024)S(1)} %bitcast.114, f32[]{:T(128)} %constant.119.clone.1, f32[7,1,2048]{0,2,1:T(8,128)S(1)} %bitcast.92, f32[2048]{0:T(1024)S(1)} %bitcast.104), kind=kCustom, calls=%fused_computation.10 | custom fusion | flops 28672 | bytes 1400836 | tf_op jit(solution)/shard_map/scatter-add | solution.py:71
  88.3 4.4 %copy.78 = f32[7,1,8,1536]{3,0,2,1:T(8,128)S(1)} copy(f32[7,1,8,1536]{0,3,2,1:T(8,128)} %bitcast.90) | data formatting | bytes 688128 | tf_op jit(solution)/shard_map/reshape | solution.py:72
  92.8 0.5 broadcast.324
  93.3 0.7 reduce.14
  94.3 1.4 copy.87
  96.0 14.8 %scatter_custom_fusion.2 = f32[2,12288]{0,1:T(8,128)} fusion(s32[2048]{0:T(1024)S(1)} %bitcast.116, f32[2048,2]{1,0:T(8,128)} %copy.87, f32[]{:T(128)} %constant.119.clone.1), kind=kCustom, calls=%fused_computation.12 | custom fusion | flops 4096 | bytes 98816 | tf_op jit(solution)/shard_map/scatter-add | solution.py:28
  110.9 0.7 pad_maximum_fusion.17
  111.6 2.1 collective-permute-start.2
  113.7 3.8 %collective-permute-start.3 = (f32[7,3,1,1536]{3,0,2,1:T(8,128)S(1)}, f32[7,3,1,1536]{3,0,2,1:T(8,128)S(1)}, u32[]{:S(2)}, u32[]{:S(2)}) collective-permute-start(f32[7,3,1,1536]{3,0,2,1:T(8,128)S(1)} %get-tuple-element.58), channel_id=1, source_target_pairs={{0,1},{1,2},{2,3},{3,4},{4,5},{5,6},{6,7},{7,8},{8,9},{9,10},{10,1... | collective-permute-start | bytes 387080 | tf_op jit(solution)/shard_map/ppermute | solution.py:16
  117.5 148.5 %all-reduce.6.cloned.1.call-done = f32[2,12288]{0,1:T(8,128)} async-done(((f32[2,12288]{0,1:T(8,128)}), f32[2,12288]{0,1:T(8,128)}) %all-reduce.6.cloned.1.call-update) | async-done | bytes 98320 | tf_op jit(solution)/shard_map/psum | solution.py:52
  266.0 9.6 %fusion = (f32[12288]{0:T(1024)S(1)}, f32[12288]{0:T(1024)S(1)}) fusion(f32[2,12288]{0,1:T(8,128)} %all-reduce.6.cloned.1.call-done, f32[]{:T(128)S(6)} %convert_element_type.52), kind=kLoop, calls=%fused_computation.5 | loop fusion | flops 24576 | bytes 196612 | tf_op jit(solution)/shard_map/mul | solution.py:122
  275.7 0.7 copy-done.3
  276.4 1.9 fusion.9
  278.3 0.6 scatter-add.33
  279.0 1.3 collective-permute-start.5
  280.3 4.0 %collective-permute-start.6 = (f32[7,1,8,1536]{3,0,2,1:T(8,128)S(1)}, f32[7,1,8,1536]{3,0,2,1:T(8,128)S(1)}, u32[]{:S(2)}, u32[]{:S(2)}) collective-permute-start(f32[7,1,8,1536]{3,0,2,1:T(8,128)S(1)} %multiply_multiply_fusion), channel_id=1, source_target_pairs={{0,32},{32,64},{64,96},{96,128},{128,160},{160,192},{192,224},{1,3... | collective-permute-start | bytes 1032200 | tf_op jit(solution)/shard_map/ppermute | solution.py:16
  284.7 4.6 %collective-permute-start.9 = (f32[7,1,2,8]{3,2,0,1:T(2,128)S(1)}, f32[7,1,2,8]{3,2,0,1:T(2,128)S(1)}, u32[]{:S(2)}, u32[]{:S(2)}) collective-permute-start(f32[7,1,2,8]{3,2,0,1:T(2,128)S(1)} %pad_maximum_fusion.19), channel_id=1, source_target_pairs={{0,256},{256,0},{1,257},{257,1},{2,258},{258,2},{3,259},{259,3},{4... | collective-permute-start | bytes 1352 | tf_op jit(solution)/shard_map/ppermute | solution.py:8
  289.3 1.6 collective-permute-done.5
  290.9 0.9 collective-permute-done.6
  291.8 0.7 pad_maximum_fusion.14
  292.5 3.8 %collective-permute-start.7 = (f32[7,3,1,1536]{3,0,2,1:T(8,128)}, f32[7,3,1,1536]{3,0,2,1:T(8,128)}, u32[]{:S(2)}, u32[]{:S(2)}) collective-permute-start(f32[7,3,1,1536]{3,0,2,1:T(8,128)} %get-tuple-element.55), channel_id=1, source_target_pairs={{1,0},{2,1},{3,2},{4,3},{5,4},{6,5},{7,6},{8,7},{9,8},{10,9},{11,1... | collective-permute-start | bytes 387080 | tf_op jit(solution)/shard_map/ppermute | solution.py:19
  296.3 3.0 collective-permute-start.8
  299.5 34.7 %all_gather.7 = f32[7,1,2,256]{0,2,1,3:T(2,128)S(1)} all-gather(f32[7,1,2,8]{0,2,1,3:T(2,128)S(1)} %copy.91), channel_id=1, replica_groups=mesh['panel'=2,'rad'=8,'ang'=32] {'ang'}, dimensions={3}, use_global_device_ids=true | all-gather | bytes 14784 | tf_op jit(solution)/shard_map/all_gather | solution.py:57
  334.3 15.5 %scatter_custom_fusion.3 = f32[7,12288]{0,1:T(8,128)} fusion(s32[2048]{0:T(1024)S(1)} %bitcast.115, f32[]{:T(128)} %constant.119.clone.1, f32[7,1,2048]{0,2,1:T(8,128)S(1)} %bitcast.91, f32[2048]{0:T(1024)S(1)} %bitcast.105), kind=kCustom, calls=%fused_computation.8 | custom fusion | flops 28672 | bytes 1400836 | tf_op jit(solution)/shard_map/scatter-add | solution.py:71
  349.8 4.4 %copy.94 = f32[7,1,8,1536]{3,0,2,1:T(8,128)S(1)} copy(f32[7,1,8,1536]{0,3,2,1:T(8,128)} %bitcast.89) | data formatting | bytes 688128 | tf_op jit(solution)/shard_map/reshape | solution.py:72
  354.3 1.6 fusion.8
  355.9 0.6 scatter-add.35
  356.6 0.9 copy.97
  (57 shorter events, 2.5 us)
Async XLA Ops:
  6.5 269.8 %copy-start = (f32[7,7]{1,0:T(8,128)S(1)}, f32[7,7]{1,0:T(8,128)}, u32[]{:S(2)}) copy-start(f32[7,7]{1,0:T(8,128)} %param.22) | copy-start | bytes 592
  7.8 103.1 %collective-permute-start = (f32[7,1,8,1536]{3,0,2,1:T(8,128)S(1)}, f32[7,1,8,1536]{3,0,2,1:T(8,128)S(1)}, u32[]{:S(2)}, u32[]{:S(2)}) collective-permute-start(f32[7,1,8,1536]{3,0,2,1:T(8,128)S(1)} %multiply_multiply_fusion.1), channel_id=1, source_target_pairs={{32,0},{64,32},{96,64},{128,96},{160,128},{192,160},{224,192},{33,... | collective-permute-start | bytes 1032200 | tf_op jit(solution)/shard_map/ppermute | solution.py:19
  9.1 101.8 %collective-permute-start.1 = (f32[7,1,8,1536]{3,0,2,1:T(8,128)S(1)}, f32[7,1,8,1536]{3,0,2,1:T(8,128)S(1)}, u32[]{:S(2)}, u32[]{:S(2)}) collective-permute-start(f32[7,1,8,1536]{3,0,2,1:T(8,128)S(1)} %multiply_multiply_fusion.1), channel_id=1, source_target_pairs={{0,32},{32,64},{64,96},{96,128},{128,160},{160,192},{192,224},{1,3... | collective-permute-start | bytes 1032200 | tf_op jit(solution)/shard_map/ppermute | solution.py:16
  14.9 22.7 %collective-permute-start.4 = (f32[7,1,2,8]{3,2,0,1:T(2,128)S(1)}, f32[7,1,2,8]{3,2,0,1:T(2,128)S(1)}, u32[]{:S(2)}, u32[]{:S(2)}) collective-permute-start(f32[7,1,2,8]{3,2,0,1:T(2,128)S(1)} %pad_maximum_fusion.18), channel_id=1, source_target_pairs={{0,256},{256,0},{1,257},{257,1},{2,258},{258,2},{3,259},{259,3},{4... | collective-permute-start | bytes 1352 | tf_op jit(solution)/shard_map/ppermute | solution.py:8
  27.3 65.4 %all-to-all-start = ((f32[32,1,192]{2,1,0:T(1,128)}), f32[32,1,192]{2,1,0:T(1,128)S(1)}, u32[]{:S(2)}, u32[]{:S(2)}) async-start(f32[32,1,192]{2,1,0:T(1,128)} %reshape.458), calls=%async_computation | async-start | bytes 65536 | tf_op jit(solution)/shard_map/all_to_all | solution.py:50
  35.9 230.2 %all-reduce.6.cloned.1.call-start = ((), (), s32[]{:S(2)}) async-start(), calls=%async_computation.1 | async-start | bytes 12582912 | tf_op jit(solution)/shard_map/psum | solution.py:52
  111.6 164.1 %collective-permute-start.2 = (f32[7,3,1,1536]{3,0,2,1:T(8,128)}, f32[7,3,1,1536]{3,0,2,1:T(8,128)S(1)}, u32[]{:S(2)}, u32[]{:S(2)}) collective-permute-start(f32[7,3,1,1536]{3,0,2,1:T(8,128)} %get-tuple-element.57), channel_id=1, source_target_pairs={{1,0},{2,1},{3,2},{4,3},{5,4},{6,5},{7,6},{8,7},{9,8},{10,9},{11,1... | collective-permute-start | bytes 387080 | tf_op jit(solution)/shard_map/ppermute | solution.py:19
  113.7 162.7 %copy-start.1 = (f32[1,7,1,8,1536]{4,3,2,1,0:T(8,128)S(1)}, f32[1,7,1,8,1536]{4,3,2,1,0:T(8,128)}, u32[]{:S(2)}) copy-start(f32[1,7,1,8,1536]{4,3,2,1,0:T(8,128)} %param.19) | copy-start | bytes 1032196
  113.7 165.2 %copy-start.2 = (f32[1,1,8,1536]{3,2,1,0:T(8,128)S(1)}, f32[1,1,8,1536]{3,2,1,0:T(8,128)}, u32[]{:S(2)}) copy-start(f32[1,1,8,1536]{3,2,1,0:T(8,128)} %param.20) | copy-start | bytes 147460
  113.7 165.2 %copy-start.4 = (f32[7]{0:T(128)S(1)}, f32[7]{0:T(128)}, u32[]{:S(2)}) copy-start(f32[7]{0:T(128)} %param.21) | copy-start | bytes 88
  113.7 162.0 %collective-permute-start.3 = (f32[7,3,1,1536]{3,0,2,1:T(8,128)S(1)}, f32[7,3,1,1536]{3,0,2,1:T(8,128)S(1)}, u32[]{:S(2)}, u32[]{:S(2)}) collective-permute-start(f32[7,3,1,1536]{3,0,2,1:T(8,128)S(1)} %get-tuple-element.58), channel_id=1, source_target_pairs={{0,1},{1,2},{2,3},{3,4},{4,5},{5,6},{6,7},{7,8},{8,9},{9,10},{10,1... | collective-permute-start | bytes 387080 | tf_op jit(solution)/shard_map/ppermute | solution.py:16
  275.7 0.7 copy-start.3
  279.0 11.9 %collective-permute-start.5 = (f32[7,1,8,1536]{3,0,2,1:T(8,128)S(1)}, f32[7,1,8,1536]{3,0,2,1:T(8,128)S(1)}, u32[]{:S(2)}, u32[]{:S(2)}) collective-permute-start(f32[7,1,8,1536]{3,0,2,1:T(8,128)S(1)} %multiply_multiply_fusion), channel_id=1, source_target_pairs={{32,0},{64,32},{96,64},{128,96},{160,128},{192,160},{224,192},{33,... | collective-permute-start | bytes 1032200 | tf_op jit(solution)/shard_map/ppermute | solution.py:19
  280.3 11.4 %collective-permute-start.6 = (f32[7,1,8,1536]{3,0,2,1:T(8,128)S(1)}, f32[7,1,8,1536]{3,0,2,1:T(8,128)S(1)}, u32[]{:S(2)}, u32[]{:S(2)}) collective-permute-start(f32[7,1,8,1536]{3,0,2,1:T(8,128)S(1)} %multiply_multiply_fusion), channel_id=1, source_target_pairs={{0,32},{32,64},{64,96},{96,128},{128,160},{160,192},{192,224},{1,3... | collective-permute-start | bytes 1032200 | tf_op jit(solution)/shard_map/ppermute | solution.py:16
  284.7 14.8 %collective-permute-start.9 = (f32[7,1,2,8]{3,2,0,1:T(2,128)S(1)}, f32[7,1,2,8]{3,2,0,1:T(2,128)S(1)}, u32[]{:S(2)}, u32[]{:S(2)}) collective-permute-start(f32[7,1,2,8]{3,2,0,1:T(2,128)S(1)} %pad_maximum_fusion.19), channel_id=1, source_target_pairs={{0,256},{256,0},{1,257},{257,1},{2,258},{258,2},{3,259},{259,3},{4... | collective-permute-start | bytes 1352 | tf_op jit(solution)/shard_map/ppermute | solution.py:8
  292.5 61.8 %collective-permute-start.7 = (f32[7,3,1,1536]{3,0,2,1:T(8,128)}, f32[7,3,1,1536]{3,0,2,1:T(8,128)}, u32[]{:S(2)}, u32[]{:S(2)}) collective-permute-start(f32[7,3,1,1536]{3,0,2,1:T(8,128)} %get-tuple-element.55), channel_id=1, source_target_pairs={{1,0},{2,1},{3,2},{4,3},{5,4},{6,5},{7,6},{8,7},{9,8},{10,9},{11,1... | collective-permute-start | bytes 387080 | tf_op jit(solution)/shard_map/ppermute | solution.py:19
  296.3 58.0 %collective-permute-start.8 = (f32[7,3,1,1536]{3,0,2,1:T(8,128)}, f32[7,3,1,1536]{3,0,2,1:T(8,128)}, u32[]{:S(2)}, u32[]{:S(2)}) collective-permute-start(f32[7,3,1,1536]{3,0,2,1:T(8,128)} %get-tuple-element.56), channel_id=1, source_target_pairs={{0,1},{1,2},{2,3},{3,4},{4,5},{5,6},{6,7},{7,8},{8,9},{9,10},{10,1... | collective-permute-start | bytes 387080 | tf_op jit(solution)/shard_map/ppermute | solution.py:16
Sparse Core Ops, SparseCore 0:
  111.0 154.9 all-reduce.5
where the time goes:
time: 365 us; the launch traced here: 364 us
  waiting for transfers between devices  151 us (41%)
  blocking collectives  69.8 us (19%)
  other arithmetic  64.2 us (18%)
  starting transfers between devices  42.5 us (12%)
  local copies, waits for them, and re-layouts  19.7 us (5%)
  between operations  13.8 us (4%)
    psum x1, waiting for transfers between devices, route_obs(): return lax.psum(dense, 'rad')  149 us
    all_gather x2, blocking collectives, other_edges(): return lax.all_gather(across, 'ang', axis=3, tiled=True)  69.8 us
    scatter-add x2, other arithmetic, ghost_terms(): target.at[:, :, flat_index]  31 us
    ppermute x4, starting transfers between devices, extended(): lax.ppermute(lax.slice_in_dim(block, block.shape[dim] - width, None, axis...  16.3 us
    scatter-add x1, other arithmetic, deposit(): return dense.at[:, cells].add(values, mode='drop')  14.8 us
    mul x1, other arithmetic, body(): forcing[moment].reshape(tile_rows, columns) * outer  9.62 us
    ppermute x2, starting transfers between devices, swapped(): lax.ppermute(x, axis, [(i, i ^ 1 << apart) for i in range(lax.axis_size(a...  9.26 us
    reshape x2, local copies, waits for them, and re-layouts, ghost_terms(): return target.reshape(fields, layers, central_rows, columns)  8.86 us
  transfers between devices with their start and end apart: 12, of which 3 were waited for; matrix products, arithmetic and copies ran while one was open for 22% of the time, Pallas kernels for 0%

commit v1 on v0

--- a/solution.py
+++ b/solution.py
@@ -54,7 +54,9 @@
 
 def other_edges(edges):
     across = swapped(edges, "panel", 0)
-    return lax.all_gather(across, "ang", axis=3, tiled=True)
+    return jnp.concatenate(
+        lax.all_to_all(jnp.stack([across] * lax.axis_size("ang")), "ang", 0, 0), axis=3
+    )
 
 
 def ghost_terms(scaled_own, row_start, central_rows, ghost_row, ghost_col, ghost_wt):

time: 365 us -> 326 us (0.89)
  blocking collectives: 69.8 us -> 0 us
  starting transfers between devices: 42.5 us -> 55.8 us
  waiting for transfers between devices: 151 us -> 164 us
  local copies, waits for them, and re-layouts: 19.7 us -> 23.5 us
    all_gather x2 -> x0, blocking collectives: 69.8 us -> none  [other_edges(): return lax.all_gather(across, 'ang', axis=3, tiled=True)]
    all_to_all x0 -> x2, starting transfers between devices: none -> 18.7 us  [other_edges(): lax.all_to_all(jnp.stack([across] * lax.axis_size('ang')), 'ang', 0, 0)]
    all_to_all x0 -> x2, waiting for transfers between devices: none -> 11.8 us  [other_edges(): lax.all_to_all(jnp.stack([across] * lax.axis_size('ang')), 'ang', 0, 0)]
    all_to_all x1, starting transfers between devices: 8.52 us -> 4.31 us  [route_obs(): lax.all_to_all(outbox, 'ang', split_axis=1, concat_axis=1, tiled=True)]
  transfers between devices with their start and end apart: 12 -> 14, of which waited for: 3 -> 4; matrix products, arithmetic and copies ran while one was open for 22% -> 26% of each run, Pallas kernels for 0% -> 0%
where the time goes in v1:
time: 326 us; the launch traced here: 325 us
  waiting for transfers between devices  164 us (50%)
  other arithmetic  64.2 us (20%)
  starting transfers between devices  55.8 us (17%)
  local copies, waits for them, and re-layouts  23.5 us (7%)
  between operations  13.8 us (4%)
  matrix products  3.43 us (1%)
    psum x1, waiting for transfers between devices, route_obs(): return lax.psum(dense, 'rad')  151 us
    scatter-add x2, other arithmetic, ghost_terms(): target.at[:, :, flat_index]  31 us
    all_to_all x2, starting transfers between devices, other_edges(): lax.all_to_all(jnp.stack([across] * lax.axis_size('ang')), 'ang', 0, 0)  18.7 us
    ppermute x4, starting transfers between devices, extended(): lax.ppermute(lax.slice_in_dim(block, block.shape[dim] - width, None, axis...  16.5 us
    scatter-add x1, other arithmetic, deposit(): return dense.at[:, cells].add(values, mode='drop')  14.8 us
    all_to_all x2, waiting for transfers between devices, other_edges(): lax.all_to_all(jnp.stack([across] * lax.axis_size('ang')), 'ang', 0, 0)  11.8 us
    mul x1, other arithmetic, body(): forcing[moment].reshape(tile_rows, columns) * outer  9.62 us
    ppermute x2, starting transfers between devices, swapped(): lax.ppermute(x, axis, [(i, i ^ 1 << apart) for i in range(lax.axis_size(a...  9.26 us
  transfers between devices with their start and end apart: 14, of which 4 were waited for; matrix products, arithmetic and copies ran while one was open for 26% of the time, Pallas kernels for 0%

profile of v1, /device:TPU:1, one launch (start us, length us, event | category | flops | bytes accessed | tf_op | source)
XLA Modules:
  0.0 325.1 jit_solution(5549235035172296309)
XLA Ops:
  6.5 1.2 multiply_multiply_fusion.1
  7.8 1.3 collective-permute-start
  9.1 5.5 %collective-permute-start.1 = (f32[7,1,8,1536]{3,0,2,1:T(8,128)S(1)}, f32[7,1,8,1536]{3,0,2,1:T(8,128)S(1)}, u32[]{:S(2)}, u32[]{:S(2)}) collective-permute-start(f32[7,1,8,1536]{3,0,2,1:T(8,128)S(1)} %multiply_multiply_fusion.1), channel_id=1, source_target_pairs={{0,32},{32,64},{64,96},{96,128},{128,160},{160,192},{192,224},{1,3... | collective-permute-start | bytes 1032200 | tf_op jit(solution)/shard_map/ppermute | solution.py:16
  14.9 4.7 %collective-permute-start.4 = (f32[7,1,2,8]{3,2,0,1:T(2,128)S(1)}, f32[7,1,2,8]{3,2,0,1:T(2,128)S(1)}, u32[]{:S(2)}, u32[]{:S(2)}) collective-permute-start(f32[7,1,2,8]{3,2,0,1:T(2,128)S(1)} %pad_maximum_fusion.18), channel_id=1, source_target_pairs={{0,256},{256,0},{1,257},{257,1},{2,258},{258,2},{3,259},{259,3},{4... | collective-permute-start | bytes 1352 | tf_op jit(solution)/shard_map/ppermute | solution.py:8
  19.8 0.7 add_select_fusion
  20.5 0.7 fusion.37
  21.2 0.6 reduce-window.6
  22.0 0.7 convert_bitcast_fusion
  22.7 0.8 fusion.36
  23.5 0.7 broadcast_multiply_fusion
  24.2 0.7 compare_select_fusion.2
  24.9 0.7 stack.9
  25.6 8.5 %all-to-all-start = ((f32[32,7,1,2,8]{4,3,2,1,0:T(2,128)}), f32[32,7,1,2,8]{4,3,2,1,0:T(2,128)S(1)}, u32[]{:S(2)}, u32[]{:S(2)}) async-start(f32[32,7,1,2,8]{4,3,2,1,0:T(2,128)} %stack.9), calls=%async_computation | async-start | bytes 458752 | tf_op jit(solution)/shard_map/all_to_all | solution.py:58
  34.2 1.0 copy.144
  35.2 1.3 scatter_fusion
  36.8 0.8 reshape.472
  37.5 7.5 %all-to-all-done = f32[32,7,1,2,8]{4,3,2,1,0:T(2,128)S(1)} async-done(((f32[32,7,1,2,8]{4,3,2,1,0:T(2,128)}), f32[32,7,1,2,8]{4,3,2,1,0:T(2,128)S(1)}, u32[]{:S(2)}, u32[]{:S(2)}) %all-to-all-start) | async-done | bytes 14368 | tf_op jit(solution)/shard_map/all_to_all | solution.py:58
  45.0 4.3 %all-to-all-start.1 = ((f32[32,1,192]{2,1,0:T(1,128)}), f32[32,1,192]{2,1,0:T(1,128)S(1)}, u32[]{:S(2)}, u32[]{:S(2)}) async-start(f32[32,1,192]{2,1,0:T(1,128)} %reshape.472), calls=%async_computation.1 | async-start | bytes 65536 | tf_op jit(solution)/shard_map/all_to_all | solution.py:50
  49.4 0.7 copy.133
  50.6 15.5 %scatter_custom_fusion = f32[7,12288]{0,1:T(8,128)} fusion(s32[2048]{0:T(1024)S(1)} %bitcast.120, f32[]{:T(128)} %constant.119.clone.1, f32[7,1,2048]{0,2,1:T(8,128)S(1)} %bitcast.96, f32[2048]{0:T(1024)S(1)} %bitcast.110), kind=kCustom, calls=%fused_computation.10 | custom fusion | flops 28672 | bytes 1400836 | tf_op jit(solution)/shard_map/scatter-add | solution.py:73
  66.1 4.4 %copy.99 = f32[7,1,8,1536]{3,0,2,1:T(8,128)S(1)} copy(f32[7,1,8,1536]{0,3,2,1:T(8,128)} %bitcast.94) | data formatting | bytes 688128 | tf_op jit(solution)/shard_map/reshape | solution.py:74
  71.1 0.7 reduce.14
  72.1 1.4 copy.108
  73.8 14.8 %scatter_custom_fusion.2 = f32[2,12288]{0,1:T(8,128)} fusion(s32[2048]{0:T(1024)S(1)} %bitcast.122, f32[2048,2]{1,0:T(8,128)} %copy.108, f32[]{:T(128)} %constant.119.clone.1), kind=kCustom, calls=%fused_computation.12 | custom fusion | flops 4096 | bytes 98816 | tf_op jit(solution)/shard_map/scatter-add | solution.py:28
  88.7 0.7 pad_maximum_fusion.17
  89.4 2.2 collective-permute-start.2
  91.7 3.6 %collective-permute-start.3 = (f32[7,3,1,1536]{3,0,2,1:T(8,128)S(1)}, f32[7,3,1,1536]{3,0,2,1:T(8,128)S(1)}, u32[]{:S(2)}, u32[]{:S(2)}) collective-permute-start(f32[7,3,1,1536]{3,0,2,1:T(8,128)S(1)} %get-tuple-element.58), channel_id=1, source_target_pairs={{0,1},{1,2},{2,3},{3,4},{4,5},{5,6},{6,7},{7,8},{8,9},{9,10},{10,1... | collective-permute-start | bytes 387080 | tf_op jit(solution)/shard_map/ppermute | solution.py:16
  95.3 151.2 %all-reduce.6.cloned.1.call-done = f32[2,12288]{0,1:T(8,128)} async-done(((f32[2,12288]{0,1:T(8,128)}), f32[2,12288]{0,1:T(8,128)}) %all-reduce.6.cloned.1.call-update) | async-done | bytes 98320 | tf_op jit(solution)/shard_map/psum | solution.py:52
  246.5 9.6 %fusion = (f32[12288]{0:T(1024)S(1)}, f32[12288]{0:T(1024)S(1)}) fusion(f32[2,12288]{0,1:T(8,128)} %all-reduce.6.cloned.1.call-done, f32[]{:T(128)S(6)} %convert_element_type.52), kind=kLoop, calls=%fused_computation.5 | loop fusion | flops 24576 | bytes 196612 | tf_op jit(solution)/shard_map/mul | solution.py:124
  256.2 0.7 copy-done.3
  256.8 1.9 fusion.9
  258.8 0.6 scatter-add.33
  259.5 1.3 collective-permute-start.5
  260.8 4.0 %collective-permute-start.6 = (f32[7,1,8,1536]{3,0,2,1:T(8,128)S(1)}, f32[7,1,8,1536]{3,0,2,1:T(8,128)S(1)}, u32[]{:S(2)}, u32[]{:S(2)}) collective-permute-start(f32[7,1,8,1536]{3,0,2,1:T(8,128)S(1)} %multiply_multiply_fusion), channel_id=1, source_target_pairs={{0,32},{32,64},{64,96},{96,128},{128,160},{160,192},{192,224},{1,3... | collective-permute-start | bytes 1032200 | tf_op jit(solution)/shard_map/ppermute | solution.py:16
  265.1 4.6 %collective-permute-start.9 = (f32[7,1,2,8]{3,2,0,1:T(2,128)S(1)}, f32[7,1,2,8]{3,2,0,1:T(2,128)S(1)}, u32[]{:S(2)}, u32[]{:S(2)}) collective-permute-start(f32[7,1,2,8]{3,2,0,1:T(2,128)S(1)} %pad_maximum_fusion.19), channel_id=1, source_target_pairs={{0,256},{256,0},{1,257},{257,1},{2,258},{258,2},{3,259},{259,3},{4... | collective-permute-start | bytes 1352 | tf_op jit(solution)/shard_map/ppermute | solution.py:8
  269.8 1.3 collective-permute-done.9
  271.0 0.7 stack.11
  271.8 10.2 %all-to-all-start.2 = ((f32[32,7,1,2,8]{4,3,2,1,0:T(2,128)}), f32[32,7,1,2,8]{4,3,2,1,0:T(2,128)S(1)}, u32[]{:S(2)}, u32[]{:S(2)}) async-start(f32[32,7,1,2,8]{4,3,2,1,0:T(2,128)} %stack.11), calls=%async_computation.2 | async-start | bytes 458752 | tf_op jit(solution)/shard_map/all_to_all | solution.py:58
  282.0 0.8 pad_maximum_fusion.14
  282.7 2.1 collective-permute-start.7
  284.9 3.4 %collective-permute-start.8 = (f32[7,3,1,1536]{3,0,2,1:T(8,128)}, f32[7,3,1,1536]{3,0,2,1:T(8,128)}, u32[]{:S(2)}, u32[]{:S(2)}) collective-permute-start(f32[7,3,1,1536]{3,0,2,1:T(8,128)} %get-tuple-element.56), channel_id=1, source_target_pairs={{0,1},{1,2},{2,3},{3,4},{4,5},{5,6},{6,7},{7,8},{8,9},{9,10},{10,1... | collective-permute-start | bytes 387080 | tf_op jit(solution)/shard_map/ppermute | solution.py:16
  288.5 4.3 %all-to-all-done.2 = f32[32,7,1,2,8]{4,3,2,1,0:T(2,128)S(1)} async-done(((f32[32,7,1,2,8]{4,3,2,1,0:T(2,128)}), f32[32,7,1,2,8]{4,3,2,1,0:T(2,128)S(1)}, u32[]{:S(2)}, u32[]{:S(2)}) %all-to-all-start.2) | async-done | bytes 14368 | tf_op jit(solution)/shard_map/all_to_all | solution.py:58
  292.8 1.1 copy.125
  294.0 1.0 mul.234
  295.0 15.5 %scatter_custom_fusion.3 = f32[7,12288]{0,1:T(8,128)} fusion(s32[2048]{0:T(1024)S(1)} %bitcast.121, f32[]{:T(128)} %constant.119.clone.1, f32[7,1,2048]{0,2,1:T(8,128)S(1)} %bitcast.95, f32[2048]{0:T(1024)S(1)} %bitcast.111), kind=kCustom, calls=%fused_computation.8 | custom fusion | flops 28672 | bytes 1400836 | tf_op jit(solution)/shard_map/scatter-add | solution.py:73
  310.5 4.4 %copy.115 = f32[7,1,8,1536]{3,0,2,1:T(8,128)S(1)} copy(f32[7,1,8,1536]{0,3,2,1:T(8,128)} %bitcast.93) | data formatting | bytes 688128 | tf_op jit(solution)/shard_map/reshape | solution.py:74
  314.9 1.6 fusion.8
  317.3 0.9 copy.118
  (59 shorter events, 4.3 us)
Async XLA Ops:
  6.5 250.3 %copy-start = (f32[7,7]{1,0:T(8,128)S(1)}, f32[7,7]{1,0:T(8,128)}, u32[]{:S(2)}) copy-start(f32[7,7]{1,0:T(8,128)} %param.22) | copy-start | bytes 592
  7.8 80.9 %collective-permute-start = (f32[7,1,8,1536]{3,0,2,1:T(8,128)S(1)}, f32[7,1,8,1536]{3,0,2,1:T(8,128)S(1)}, u32[]{:S(2)}, u32[]{:S(2)}) collective-permute-start(f32[7,1,8,1536]{3,0,2,1:T(8,128)S(1)} %multiply_multiply_fusion.1), channel_id=1, source_target_pairs={{32,0},{64,32},{96,64},{128,96},{160,128},{192,160},{224,192},{33,... | collective-permute-start | bytes 1032200 | tf_op jit(solution)/shard_map/ppermute | solution.py:19
  9.1 79.6 %collective-permute-start.1 = (f32[7,1,8,1536]{3,0,2,1:T(8,128)S(1)}, f32[7,1,8,1536]{3,0,2,1:T(8,128)S(1)}, u32[]{:S(2)}, u32[]{:S(2)}) collective-permute-start(f32[7,1,8,1536]{3,0,2,1:T(8,128)S(1)} %multiply_multiply_fusion.1), channel_id=1, source_target_pairs={{0,32},{32,64},{64,96},{96,128},{128,160},{160,192},{192,224},{1,3... | collective-permute-start | bytes 1032200 | tf_op jit(solution)/shard_map/ppermute | solution.py:16
  14.9 10.0 %collective-permute-start.4 = (f32[7,1,2,8]{3,2,0,1:T(2,128)S(1)}, f32[7,1,2,8]{3,2,0,1:T(2,128)S(1)}, u32[]{:S(2)}, u32[]{:S(2)}) collective-permute-start(f32[7,1,2,8]{3,2,0,1:T(2,128)S(1)} %pad_maximum_fusion.18), channel_id=1, source_target_pairs={{0,256},{256,0},{1,257},{257,1},{2,258},{258,2},{3,259},{259,3},{4... | collective-permute-start | bytes 1352 | tf_op jit(solution)/shard_map/ppermute | solution.py:8
  25.6 19.4 %all-to-all-start = ((f32[32,7,1,2,8]{4,3,2,1,0:T(2,128)}), f32[32,7,1,2,8]{4,3,2,1,0:T(2,128)S(1)}, u32[]{:S(2)}, u32[]{:S(2)}) async-start(f32[32,7,1,2,8]{4,3,2,1,0:T(2,128)} %stack.9), calls=%async_computation | async-start | bytes 458752 | tf_op jit(solution)/shard_map/all_to_all | solution.py:58
  45.0 25.5 %all-to-all-start.1 = ((f32[32,1,192]{2,1,0:T(1,128)}), f32[32,1,192]{2,1,0:T(1,128)S(1)}, u32[]{:S(2)}, u32[]{:S(2)}) async-start(f32[32,1,192]{2,1,0:T(1,128)} %reshape.472), calls=%async_computation.1 | async-start | bytes 65536 | tf_op jit(solution)/shard_map/all_to_all | solution.py:50
  49.3 197.2 %all-reduce.6.cloned.1.call-start = ((), (), s32[]{:S(2)}) async-start(), calls=%async_computation.3 | async-start | bytes 12582912 | tf_op jit(solution)/shard_map/psum | solution.py:52
  89.4 166.7 %collective-permute-start.2 = (f32[7,3,1,1536]{3,0,2,1:T(8,128)}, f32[7,3,1,1536]{3,0,2,1:T(8,128)S(1)}, u32[]{:S(2)}, u32[]{:S(2)}) collective-permute-start(f32[7,3,1,1536]{3,0,2,1:T(8,128)} %get-tuple-element.57), channel_id=1, source_target_pairs={{1,0},{2,1},{3,2},{4,3},{5,4},{6,5},{7,6},{8,7},{9,8},{10,9},{11,1... | collective-permute-start | bytes 387080 | tf_op jit(solution)/shard_map/ppermute | solution.py:19
  91.6 165.2 %copy-start.1 = (f32[1,7,1,8,1536]{4,3,2,1,0:T(8,128)S(1)}, f32[1,7,1,8,1536]{4,3,2,1,0:T(8,128)}, u32[]{:S(2)}) copy-start(f32[1,7,1,8,1536]{4,3,2,1,0:T(8,128)} %param.19) | copy-start | bytes 1032196
  91.7 167.7 %copy-start.2 = (f32[1,1,8,1536]{3,2,1,0:T(8,128)S(1)}, f32[1,1,8,1536]{3,2,1,0:T(8,128)}, u32[]{:S(2)}) copy-start(f32[1,1,8,1536]{3,2,1,0:T(8,128)} %param.20) | copy-start | bytes 147460
  91.7 167.7 %copy-start.4 = (f32[7]{0:T(128)S(1)}, f32[7]{0:T(128)}, u32[]{:S(2)}) copy-start(f32[7]{0:T(128)} %param.21) | copy-start | bytes 88
  91.7 164.5 %collective-permute-start.3 = (f32[7,3,1,1536]{3,0,2,1:T(8,128)S(1)}, f32[7,3,1,1536]{3,0,2,1:T(8,128)S(1)}, u32[]{:S(2)}, u32[]{:S(2)}) collective-permute-start(f32[7,3,1,1536]{3,0,2,1:T(8,128)S(1)} %get-tuple-element.58), channel_id=1, source_target_pairs={{0,1},{1,2},{2,3},{3,4},{4,5},{5,6},{6,7},{7,8},{8,9},{9,10},{10,1... | collective-permute-start | bytes 387080 | tf_op jit(solution)/shard_map/ppermute | solution.py:16
  256.1 0.7 copy-start.3
  259.5 22.5 %collective-permute-start.5 = (f32[7,1,8,1536]{3,0,2,1:T(8,128)S(1)}, f32[7,1,8,1536]{3,0,2,1:T(8,128)S(1)}, u32[]{:S(2)}, u32[]{:S(2)}) collective-permute-start(f32[7,1,8,1536]{3,0,2,1:T(8,128)S(1)} %multiply_multiply_fusion), channel_id=1, source_target_pairs={{32,0},{64,32},{96,64},{128,96},{160,128},{192,160},{224,192},{33,... | collective-permute-start | bytes 1032200 | tf_op jit(solution)/shard_map/ppermute | solution.py:19
  260.8 21.2 %collective-permute-start.6 = (f32[7,1,8,1536]{3,0,2,1:T(8,128)S(1)}, f32[7,1,8,1536]{3,0,2,1:T(8,128)S(1)}, u32[]{:S(2)}, u32[]{:S(2)}) collective-permute-start(f32[7,1,8,1536]{3,0,2,1:T(8,128)S(1)} %multiply_multiply_fusion), channel_id=1, source_target_pairs={{0,32},{32,64},{64,96},{96,128},{128,160},{160,192},{192,224},{1,3... | collective-permute-start | bytes 1032200 | tf_op jit(solution)/shard_map/ppermute | solution.py:16
  265.1 5.9 %collective-permute-start.9 = (f32[7,1,2,8]{3,2,0,1:T(2,128)S(1)}, f32[7,1,2,8]{3,2,0,1:T(2,128)S(1)}, u32[]{:S(2)}, u32[]{:S(2)}) collective-permute-start(f32[7,1,2,8]{3,2,0,1:T(2,128)S(1)} %pad_maximum_fusion.19), channel_id=1, source_target_pairs={{0,256},{256,0},{1,257},{257,1},{2,258},{258,2},{3,259},{259,3},{4... | collective-permute-start | bytes 1352 | tf_op jit(solution)/shard_map/ppermute | solution.py:8
  271.8 21.0 %all-to-all-start.2 = ((f32[32,7,1,2,8]{4,3,2,1,0:T(2,128)}), f32[32,7,1,2,8]{4,3,2,1,0:T(2,128)S(1)}, u32[]{:S(2)}, u32[]{:S(2)}) async-start(f32[32,7,1,2,8]{4,3,2,1,0:T(2,128)} %stack.11), calls=%async_computation.2 | async-start | bytes 458752 | tf_op jit(solution)/shard_map/all_to_all | solution.py:58
  282.7 32.2 %collective-permute-start.7 = (f32[7,3,1,1536]{3,0,2,1:T(8,128)}, f32[7,3,1,1536]{3,0,2,1:T(8,128)}, u32[]{:S(2)}, u32[]{:S(2)}) collective-permute-start(f32[7,3,1,1536]{3,0,2,1:T(8,128)} %get-tuple-element.55), channel_id=1, source_target_pairs={{1,0},{2,1},{3,2},{4,3},{5,4},{6,5},{7,6},{8,7},{9,8},{10,9},{11,1... | collective-permute-start | bytes 387080 | tf_op jit(solution)/shard_map/ppermute | solution.py:19
  284.9 30.0 %collective-permute-start.8 = (f32[7,3,1,1536]{3,0,2,1:T(8,128)}, f32[7,3,1,1536]{3,0,2,1:T(8,128)}, u32[]{:S(2)}, u32[]{:S(2)}) collective-permute-start(f32[7,3,1,1536]{3,0,2,1:T(8,128)} %get-tuple-element.56), channel_id=1, source_target_pairs={{0,1},{1,2},{2,3},{3,4},{4,5},{5,6},{6,7},{7,8},{8,9},{9,10},{10,1... | collective-permute-start | bytes 387080 | tf_op jit(solution)/shard_map/ppermute | solution.py:16
Sparse Core Ops, SparseCore 0:
  88.8 157.6 all-reduce.5
